TPU v7x, 32 devices: a whole 2x2x4 slice. The times are simulated.
32 devices in a mesh: prow: 4 (over y, core), pcol: 8 (over z, x).
Axes of the slice: x: 2, y: 2, z: 4, core: 2. Of those that a mesh axis runs over, the one named last changes fastest.
Arguments:
- ainv_trail: float32 [2048, 2048], P('prow', 'pcol')
- panel_parent: float32 [2048, 256], P('prow', 'pcol'), may hold values from -0.125 to 0.125
- panel_child: float32 [2048, 256], P('prow', 'pcol'), may hold values from -0.125 to 0.125
- link_block: float32 [256, 256], replicated, may hold values from -0.375 to 0.375
- dinv_parent: float32 [256, 256], replicated
- dinv_child: float32 [256, 256], replicated
- pattern_parent: int32 [8], replicated, may hold values from 0 to 1, as said below
- pattern_child: int32 [8], replicated, may hold values from 0 to 1, as said below
Outputs:
- row_parent: float32 [256, 2048], P('prow', 'pcol')
- diag_parent: float32 [256, 256], P('prow')
- cross_child: float32 [256, 256], P('prow')
- row_child: float32 [256, 2048], P('prow', 'pcol')
- diag_child: float32 [256, 256], P('prow')
Inputs may be any that keep to these rules, and one draw needn't show every extreme that they name: `pattern_parent`: each entry is 0 or 1; the first entry is 1 and at least one entry is 0. `pattern_child`: each entry is 0 or 1, and is 1 only where pattern_parent is 1; the first entry is 1.
All inputs are finite; a program needn't handle non-finite values.
Results may differ from a plain program's by a relative error of at most 0.00009.
Values sent between devices are 32-bit elements; how exact they have to be, the bound alone decides.
A program may use at most 64 MiB of HBM per device.

v0:
```python
import jax
import jax.numpy as jnp
from jax import lax
from jax.sharding import PartitionSpec as P

highest = lax.Precision.HIGHEST


def lead_product(left, right):
    return lax.dot_general(
        left, right, (((0,), (0,)), ((), ())), precision=highest, preferred_element_type=jnp.float32
    )


def plain_product(left, right):
    return jnp.dot(left, right, precision=highest, preferred_element_type=jnp.float32)


def block_mask(pattern, first, count, width):
    picked = lax.dynamic_slice(pattern, (first,), (count,)).astype(jnp.float32)
    return jnp.repeat(picked, width)


def row_total(partial_value, columns, row_index, share):
    total = lax.psum(partial_value, "prow")
    whole = -total * columns[None, :]
    return (lax.dynamic_slice_in_dim(whole, row_index * share, share, 0), whole)


def total_terms(stacked):
    return lax.psum(stacked, ("prow", "pcol"))


def column_terms(row_part, blocks):
    result = plain_product(row_part, blocks[0])
    return result


def on_device(
    ainv_trail,
    panel_parent,
    panel_child,
    link_block,
    dinv_parent,
    dinv_child,
    pattern_parent,
    pattern_child,
):
    width = link_block.shape[0]
    row_count = lax.axis_size("prow")
    row_index = lax.axis_index("prow")
    col_index = lax.axis_index("pcol")
    row_blocks = ainv_trail.shape[0] // width
    col_blocks = ainv_trail.shape[1] // width
    share = width // row_count
    first_row = row_index * row_blocks
    first_col = col_index * col_blocks
    parent_whole, child_whole = (
        lax.all_gather(panel_parent, "pcol", axis=1, tiled=True),
        lax.all_gather(panel_child, "pcol", axis=1, tiled=True),
    )
    parent_rows = parent_whole * block_mask(pattern_parent, first_row, row_blocks, width)[:, None]
    child_rows = child_whole * block_mask(pattern_child, first_row, row_blocks, width)[:, None]
    parent_cols = block_mask(pattern_parent, first_col, col_blocks, width)
    child_cols = block_mask(pattern_child, first_col, col_blocks, width)
    parent_partial = lead_product(parent_rows, ainv_trail)
    child_partial = lead_product(child_rows, ainv_trail)
    link_share = lax.dynamic_slice_in_dim(link_block, row_index * share, share, 0)
    block = first_col + 0
    root = block // row_blocks
    local = jnp.clip(block - first_row, 0, row_blocks - 1)
    parent_piece = lax.dynamic_slice_in_dim(parent_rows, local * width, width, 0)
    child_piece = lax.dynamic_slice_in_dim(child_rows, local * width, width, 0)
    owner = (root == row_index).astype(jnp.float32)
    parent_piece = parent_piece * owner
    child_piece = child_piece * owner
    parent_blocks = [parent_piece]
    child_blocks = [child_piece]
    parent_share, parent_part = row_total(parent_partial, parent_cols, row_index, share)
    first_terms = total_terms(
        jnp.stack(
            [column_terms(parent_part, parent_blocks), column_terms(parent_part, child_blocks)]
        )
    )
    diag_parent = dinv_parent - first_terms[0]
    cross_child = -(lead_product(link_block, diag_parent) + first_terms[1].T)
    child_partial = child_partial + lead_product(link_share, parent_share)
    child_share, child_part = row_total(child_partial, child_cols, row_index, share)
    second_terms = total_terms(jnp.stack([column_terms(child_part, child_blocks)]))
    diag_child = dinv_child - plain_product(cross_child, link_block) - second_terms[0]
    start = row_index * share
    return (
        parent_share,
        lax.dynamic_slice_in_dim(diag_parent, start, share, 0),
        lax.dynamic_slice_in_dim(cross_child, start, share, 0),
        child_share,
        lax.dynamic_slice_in_dim(diag_child, start, share, 0),
    )


def solution(mesh):
    return jax.shard_map(
        on_device,
        mesh=mesh,
        in_specs=(P("prow", "pcol"), P("prow", "pcol"), P("prow", "pcol"), P(), P(), P(), P(), P()),
        out_specs=(
            P("prow", "pcol"),
            P("prow", None),
            P("prow", None),
            P("prow", "pcol"),
            P("prow", None),
        ),
        check_vma=False,
    )
```

profile of v0, /device:TPU:0, one launch (start us, length us, event | category | flops | bytes accessed | tf_op | source)
XLA Modules:
  0.0 260.4 jit_solution(992268018349741853)
XLA Ops:
  7.3 0.7 copy-done.6
  8.0 0.1 dynamic-slice_convert_fusion
  8.0 0.1 broadcast_bitcast_fusion.1
  8.1 33.2 %all_gather.6 = f32[512,256]{0,1:T(8,128)S(1)} all-gather(f32[512,32]{0,1:T(8,128)} %param.9), channel_id=1, replica_groups=mesh['prow'=4,'pcol'=8] {'pcol'}, dimensions={1}, use_global_device_ids=true | all-gather | bytes 589824 | tf_op jit(solution)/shard_map/all_gather | solution.py:59
  41.4 0.1 broadcast_multiply_fusion.1
  41.4 1.3 fusion.13
  42.8 0.0 all-reduce.7.cloned.1.call-start
  42.8 0.6 dynamic_slice.45
  43.4 0.6 dynamic_slice.37
  45.3 0.1 broadcast_bitcast_fusion
  45.4 31.2 %all_gather.7 = f32[512,256]{0,1:T(8,128)S(1)} all-gather(f32[512,32]{0,1:T(8,128)S(1)} %copy-done.5), channel_id=1, replica_groups=mesh['prow'=4,'pcol'=8] {'pcol'}, dimensions={1}, use_global_device_ids=true | all-gather | bytes 589824 | tf_op jit(solution)/shard_map/all_gather | solution.py:60
  76.6 0.1 broadcast_multiply_fusion
  76.6 0.6 fusion.14
  77.3 1.0 negate_multiply_fusion.1
  78.3 1.1 convolution_add_fusion
  79.5 0.0 all-reduce.9.cloned.1.call-start
  79.5 0.4 convolution_bitcast_fusion.1
  80.0 0.4 convolution_bitcast_fusion
  80.4 0.8 pad_maximum_fusion
  81.2 32.0 %all-reduce.7.cloned.1.call-done = f32[256,256]{1,0:T(8,128)} async-done(((f32[256,256]{1,0:T(8,128)}), f32[256,256]{1,0:T(8,128)}) %all-reduce.7.cloned.1.call-update) | async-done | bytes 262160 | tf_op jit(solution)/shard_map/psum | solution.py:25
  113.2 1.0 negate_multiply_fusion
  114.2 1.1 fusion.4
  115.3 0.6 constant_dynamic-slice_fusion
  116.0 132.6 %all-reduce.9.cloned.1.call-done = (f32[2,256,256]{2,1,0:T(8,128)}, f32[256,256]{1,0:T(8,128)}) async-done(((f32[2,256,256]{2,1,0:T(8,128)}, f32[256,256]{1,0:T(8,128)}), (f32[2,256,256]{2,1,0:T(8,128)}, f32[256,256]{1,0:T(8,128)})) %all-reduce.9.cloned.1.call-update) | async-done | bytes 786448 | tf_op jit(solution)/shard_map/psum | solution.py:31
  248.6 1.1 fusion.1
  249.6 0.1 copy-done.2
  249.7 0.6 fusion
  250.3 0.6 constant_dynamic-slice_fusion.1
  250.9 0.1 dynamic-slice_bitcast_fusion
  251.0 0.6 fusion.15
  251.6 0.7 copy.14
  252.3 1.5 dynamic-slice_subtract_fusion
  (22 shorter events, 0.2 us)
Async XLA Ops:
  7.2 34.3 %copy-start = (f32[512,256]{1,0:T(8,128)S(1)}, f32[512,256]{1,0:T(8,128)}, u32[]{:S(2)}) copy-start(f32[512,256]{1,0:T(8,128)} %param.8) | copy-start | bytes 1572868
  7.2 70.1 %all-reduce.5.cloned.1.call-start = ((), (), s32[]{:S(2)}) async-start(), calls=%async_computation | async-start | bytes 524288 | tf_op jit(solution)/shard_map/psum | solution.py:25
  7.2 0.7 copy-start.6
  7.2 0.7 copy-start.7
  42.7 2.6 %copy-start.5 = (f32[512,32]{0,1:T(8,128)S(1)}, f32[512,32]{0,1:T(8,128)}, u32[]{:S(2)}) copy-start(f32[512,32]{0,1:T(8,128)} %param.10) | copy-start | bytes 196612
  42.8 70.5 %all-reduce.7.cloned.1.call-start = ((), (), s32[]{:S(2)}) async-start(), calls=%async_computation.1 | async-start | bytes 524288 | tf_op jit(solution)/shard_map/psum | solution.py:25
  77.2 1.1 copy-start.1
  78.3 1.1 copy-start.4
  79.5 169.1 %all-reduce.9.cloned.1.call-start = ((), (), s32[]{:S(2)}) async-start(), calls=%async_computation.2 | async-start | bytes 1572864 | tf_op jit(solution)/shard_map/psum | solution.py:31
  115.3 133.3 %copy-start.3 = (f32[256,256]{1,0:T(8,128)S(1)}, f32[256,256]{1,0:T(8,128)}, u32[]{:S(2)}) copy-start(f32[256,256]{1,0:T(8,128)} %param.12) | copy-start | bytes 786436
  248.6 1.1 copy-start.2
Sparse Core Ops, SparseCore 0:
  42.9 33.3 all-reduce.4
  79.6 33.5 all-reduce.6
  118.5 130.0 all-reduce.8
where the time goes:
time: 261 us; the launch traced here: 260 us
  waiting for transfers between devices  165 us (63%)
  blocking collectives  64.4 us (25%)
  between operations  15.2 us (6%)
  matrix products  6.15 us (2%)
  other arithmetic  5.56 us (2%)
  local copies, waits for them, and re-layouts  4.23 us (2%)
    psum x1, waiting for transfers between devices, total_terms(): return lax.psum(stacked, ('prow', 'pcol'))  133 us
    all_gather x1, blocking collectives, on_device(): lax.all_gather(panel_parent, 'pcol', axis=1, tiled=True)  33.2 us
    psum x2, waiting for transfers between devices, row_total(): total = lax.psum(partial_value, 'prow')  32 us
    all_gather x1, blocking collectives, on_device(): lax.all_gather(panel_child, 'pcol', axis=1, tiled=True)  31.2 us
  transfers between devices with their start and end apart: 3, of which 2 were waited for; matrix products, arithmetic and copies ran while one was open for 2% of the time, Pallas kernels for 0%

commit v1 on v0

--- a/solution.py
+++ b/solution.py
@@ -1,7 +1,13 @@
+import functools
+
 import jax
 import jax.numpy as jnp
 from jax import lax
+from jax.experimental import pallas as pl
+from jax.experimental.pallas import tpu as pltpu
 from jax.sharding import PartitionSpec as P
+
+MESH = pl.DeviceIdType.MESH
 
 highest = lax.Precision.HIGHEST
 
@@ -98,9 +104,357 @@
     )
 
 
+def halves(value):
+    high = value.astype(jnp.bfloat16)
+    return high, (value - high.astype(jnp.float32)).astype(jnp.bfloat16)
+
+
+def product(left, right, left_dim, right_dim):
+    dims = (((left_dim,), (right_dim,)), ((), ()))
+    (left_high, left_low), (right_high, right_low) = left, right
+
+    def one(a, b):
+        return lax.dot_general(a, b, dims, preferred_element_type=jnp.float32)
+
+    return one(left_high, right_high) + (one(left_high, right_low) + one(left_low, right_high))
+
+
+def kernel(
+    rows,
+    cols,
+    pattern_parent,
+    pattern_child,
+    piece,
+    ainv,
+    link,
+    dinv_parent,
+    dinv_child,
+    row_parent,
+    diag_parent,
+    cross_child,
+    row_child,
+    diag_child,
+    panel,
+    block_panel,
+    ainv_high,
+    ainv_low,
+    masks,
+    partial,
+    arrived,
+    terms,
+    term_slots,
+    finals,
+    link_dinv,
+    up_sem,
+    down_sem,
+    side_sem,
+    panel_sem,
+    own_sem,
+    spread_sem,
+    block_sem,
+    share_send,
+    share_recv,
+    term_send,
+    term_recv,
+    final_send,
+    final_recv,
+):
+    i, j = lax.axis_index("prow"), lax.axis_index("pcol")
+    z, x = j // 2, j % 2
+    depth = cols // 2
+    width = link.shape[0]
+    piece_rows = piece.shape[1]
+    blocks = ainv.shape[0] // width
+    share = width // rows
+    own = share // cols
+    other_x = 1 - x
+
+    far = z // (depth // 2)
+    near = z + far * (depth - 1 - 2 * z)
+    steps = [near, 1 - near] + list(range(2, depth))
+    levels = [s + far * (depth - 1 - 2 * s) for s in steps]
+
+    def piece_of(level, side):
+        start = pl.multiple_of((level * 2 + side) * piece_rows, piece_rows)
+        return panel.at[:, pl.ds(start, piece_rows), :]
+
+    def to(source, level, side, sem, device):
+        return pltpu.make_async_remote_copy(
+            src_ref=source,
+            dst_ref=piece_of(level, side),
+            send_sem=sem,
+            recv_sem=panel_sem.at[level * 2 + side],
+            device_id=device,
+            device_id_type=MESH,
+        )
+
+    def up(source, level):
+        return to(source, level, x, up_sem.at[level], (i, jnp.minimum(j + 2, cols - 1)))
+
+    def down(source, level):
+        return to(source, level, x, down_sem.at[level], (i, jnp.maximum(j - 2, 0)))
+
+    def side(source, level):
+        return to(source, level, x, side_sem.at[level], (i, z * 2 + other_x))
+
+    def relay(source, level, act):
+        @pl.when(jnp.logical_and(level <= z, z < depth - 1))
+        def _():
+            act(up(source, level))
+
+        @pl.when(jnp.logical_and(level >= z, z > 0))
+        def _():
+            act(down(source, level))
+
+        act(side(source, level))
+
+    def start(copy):
+        copy.start()
+
+    owner = j // blocks
+    half = pl.multiple_of((j % blocks) * width, width)
+
+    def spread_copy(slot, k):
+        begin = pl.multiple_of(slot * piece_rows, piece_rows)
+        return pltpu.make_async_remote_copy(
+            src_ref=panel.at[:, pl.ds(begin, piece_rows), pl.ds(half, width)],
+            dst_ref=block_panel.at[:, pl.ds(begin, piece_rows), :],
+            send_sem=spread_sem.at[slot, k],
+            recv_sem=block_sem.at[slot],
+            device_id=((i + 1 + k) % rows, j),
+            device_id_type=MESH,
+        )
+
+    def keep_copy(slot):
+        begin = pl.multiple_of(slot * piece_rows, piece_rows)
+        return pltpu.make_async_copy(
+            panel.at[:, pl.ds(begin, piece_rows), pl.ds(half, width)],
+            block_panel.at[:, pl.ds(begin, piece_rows), :],
+            block_sem.at[slot],
+        )
+
+    barrier = pltpu.get_barrier_semaphore()
+    for k in range(1, cols):
+        pl.semaphore_signal(barrier, inc=1, device_id=(i, (j + k) % cols), device_id_type=MESH)
+    for k in range(1, rows):
+        pl.semaphore_signal(barrier, inc=1, device_id=((i + k) % rows, j), device_id_type=MESH)
+    keep_own = pltpu.make_async_copy(piece, piece_of(z, x), own_sem)
+    keep_own.start()
+    high, low = halves(ainv[...])
+    ainv_high[...] = high
+    ainv_low[...] = low
+    for b in range(blocks):
+        for p, pattern in enumerate((pattern_parent, pattern_child)):
+            value = pattern[i * blocks + b].astype(jnp.float32)
+            masks[p, :, b * width : (b + 1) * width] = jnp.full((piece_rows, width), 1.0, jnp.float32) * value
+    pl.semaphore_wait(barrier, cols - 1 + rows - 1)
+    relay(piece, z, start)
+
+    def take(level, side_index):
+        slot = level * 2 + side_index
+
+        @pl.when(i == owner)
+        def _():
+            for k in range(rows - 1):
+                spread_copy(slot, k).start()
+            keep_copy(slot).start()
+
+        begin = pl.multiple_of(slot * piece_rows, piece_rows)
+        value = panel[:, pl.ds(begin, piece_rows), :] * masks[...]
+        value = value.reshape(2 * piece_rows, value.shape[2])
+        value_high, value_low = halves(value)
+        both = jnp.concatenate([value_high, value_low], axis=0)
+        first = jnp.dot(both, ainv_high[...], preferred_element_type=jnp.float32)
+        second = jnp.dot(value_high, ainv_low[...], preferred_element_type=jnp.float32)
+        total = first[: 2 * piece_rows] + first[2 * piece_rows :] + second
+        partial[0, pl.ds(begin, piece_rows), :] = total[:piece_rows]
+        partial[1, pl.ds(begin, piece_rows), :] = total[piece_rows:]
+
+    link_halves = halves(link[...])
+    link_dinv[...] = product(link_halves, halves(dinv_parent[...]), 0, 0)
+
+    keep_own.wait()
+    take(z, x)
+    for k in range(1, depth + 1):
+        if k < depth:
+            level = levels[k]
+            to(piece, level, x, own_sem, (i, z * 2 + other_x)).wait_recv()
+            relay(piece_of(level, x), level, start)
+            take(level, x)
+        level = levels[k - 1]
+        to(piece, level, other_x, own_sem, (i, z * 2 + other_x)).wait_recv()
+        take(level, other_x)
+
+    def share_copy(p, k):
+        target = (i + k) % rows
+        begin = pl.multiple_of(target * share, share)
+        return pltpu.make_async_remote_copy(
+            src_ref=partial.at[p, pl.ds(begin, share), :],
+            dst_ref=arrived.at[p, k - 1],
+            send_sem=share_send.at[p, k - 1],
+            recv_sem=share_recv.at[p, k - 1],
+            device_id=(target, j),
+            device_id_type=MESH,
+        )
+
+    for k in (2, 1, 3):
+        share_copy(0, k).start()
+    partial[1] = partial[1] - product(link_halves, halves(partial[0]), 0, 0)
+    for k in (2, 1, 3):
+        share_copy(1, k).start()
+
+    parent_here = pattern_parent[j].astype(jnp.float32)
+    child_here = pattern_child[j].astype(jnp.float32)
+    for slot in range(cols):
+        keep_copy(slot).wait()
+    parent_block = halves(block_panel[0])
+    child_block = halves(block_panel[1])
+
+    mine = pl.multiple_of(i * share, share)
+    sums = []
+    for p in range(2):
+        total = partial[p, pl.ds(mine, share), :]
+        for k in range(1, rows):
+            share_copy(p, k).wait_recv()
+            total = total + arrived[p, k - 1]
+        sums.append(-total)
+    parent_sum, child_sum = sums
+    parent_sum = parent_sum * parent_here
+    row_parent[...] = parent_sum
+    row_child[...] = child_sum * child_here
+
+    parent_terms = product(halves(jnp.concatenate([parent_sum, child_sum], axis=0)), parent_block, 1, 1)
+    parent_terms = parent_terms * parent_here
+    child_terms = product(halves(child_sum), child_block, 1, 1) * child_here
+    terms[0] = parent_terms[:share]
+    terms[1] = parent_terms[share:]
+    terms[2] = child_terms
+
+    def term_copy(k):
+        target = (j + k) % cols
+        begin = pl.multiple_of(target * own, own)
+        return pltpu.make_async_remote_copy(
+            src_ref=terms.at[:, pl.ds(begin, own), :],
+            dst_ref=term_slots.at[k - 1],
+            send_sem=term_send.at[k - 1],
+            recv_sem=term_recv.at[k - 1],
+            device_id=(i, target),
+            device_id_type=MESH,
+        )
+
+    for k in range(1, cols):
+        term_copy(k).start()
+    begin = pl.multiple_of(j * own, own)
+    place = pl.multiple_of(mine + begin, own)
+    total = terms[:, pl.ds(begin, own), :]
+    for k in range(1, cols):
+        term_copy(k).wait_recv()
+        total = total + term_slots[k - 1]
+    cross = -(link_dinv[pl.ds(place, own), :] + total[1])
+    finals[0, pl.ds(begin, own), :] = dinv_parent[pl.ds(place, own), :] - total[0]
+    finals[1, pl.ds(begin, own), :] = cross
+    finals[2, pl.ds(begin, own), :] = (
+        dinv_child[pl.ds(place, own), :] - product(halves(cross), link_halves, 1, 0) - total[2]
+    )
+
+    def final_copy(k, origin):
+        at = finals.at[:, pl.ds(pl.multiple_of(origin * own, own), own), :]
+        return pltpu.make_async_remote_copy(
+            src_ref=at,
+            dst_ref=at,
+            send_sem=final_send.at[k - 1],
+            recv_sem=final_recv.at[k - 1],
+            device_id=(i, (j + k) % cols),
+            device_id_type=MESH,
+        )
+
+    for k in range(1, cols):
+        final_copy(k, j).start()
+
+    for k in range(depth):
+        relay(piece_of(levels[k], x), levels[k], lambda copy: copy.wait_send())
+
+    @pl.when(i == owner)
+    def _():
+        for slot in range(cols):
+            for k in range(rows - 1):
+                spread_copy(slot, k).wait_send()
+
+    for p in range(2):
+        for k in range(1, rows):
+            share_copy(p, k).wait_send()
+    for k in range(1, cols):
+        term_copy(k).wait_send()
+    for k in range(1, cols):
+        final_copy(k, (j + cols - k) % cols).wait_recv()
+    diag_parent[...] = finals[0]
+    cross_child[...] = finals[1]
+    diag_child[...] = finals[2]
+    for k in range(1, cols):
+        final_copy(k, j).wait_send()
+
+
+def fused(rows, cols, ainv, parent, child, link, dinv_parent, dinv_child, pattern_parent, pattern_child):
+    width = link.shape[0]
+    share = width // rows
+    own = share // cols
+    piece = jnp.stack([parent.T, child.T])
+    piece_rows, height = piece.shape[1:]
+    f32 = jnp.float32
+    dma = pltpu.SemaphoreType.DMA
+    vmem = pl.BlockSpec(memory_space=pltpu.VMEM)
+    smem = pl.BlockSpec(memory_space=pltpu.SMEM)
+    wide = jax.ShapeDtypeStruct((share, width), f32)
+    return pl.pallas_call(
+        functools.partial(kernel, rows, cols),
+        out_shape=(wide,) * 5,
+        in_specs=[smem, smem] + [vmem] * 5,
+        out_specs=(vmem,) * 5,
+        scratch_shapes=[
+            pltpu.VMEM((2, width, height), f32),
+            pltpu.VMEM((2, width, width), f32),
+            pltpu.VMEM((height, width), jnp.bfloat16),
+            pltpu.VMEM((height, width), jnp.bfloat16),
+            pltpu.VMEM((2, piece_rows, height), f32),
+            pltpu.VMEM((2, width, width), f32),
+            pltpu.VMEM((2, rows - 1, share, width), f32),
+            pltpu.VMEM((3, share, width), f32),
+            pltpu.VMEM((cols - 1, 3, own, width), f32),
+            pltpu.VMEM((3, share, width), f32),
+            pltpu.VMEM((width, width), f32),
+            dma((cols // 2,)),
+            dma((cols // 2,)),
+            dma((cols // 2,)),
+            dma((cols,)),
+            dma,
+            dma((cols, rows - 1)),
+            dma((cols,)),
+            dma((2, rows - 1)),
+            dma((2, rows - 1)),
+            dma((cols - 1,)),
+            dma((cols - 1,)),
+            dma((cols - 1,)),
+            dma((cols - 1,)),
+        ],
+        compiler_params=pltpu.CompilerParams(collective_id=0, has_side_effects=True),
+    )(pattern_parent, pattern_child, piece, ainv, link, dinv_parent, dinv_child)
+
+
+def fits(rows, cols, width):
+    return cols == 8 and width % (rows * cols * 8) == 0
+
+
 def solution(mesh):
+    rows, cols = mesh.shape["prow"], mesh.shape["pcol"]
+
+    def step(ainv, parent, child, link, *rest):
+        plain = ainv.shape[1] == link.shape[0] and parent.shape[1] % 8 == 0
+        if plain and fits(rows, cols, link.shape[0]):
+            return fused(rows, cols, ainv, parent, child, link, *rest)
+        return on_device(ainv, parent, child, link, *rest)
+
     return jax.shard_map(
-        on_device,
+        step,
         mesh=mesh,
         in_specs=(P("prow", "pcol"), P("prow", "pcol"), P("prow", "pcol"), P(), P(), P(), P(), P()),
         out_specs=(

time: 261 us -> 51.5 us (0.20)
  waiting for transfers between devices: 165 us -> 0 us
  blocking collectives: 64.4 us -> 0 us
  Pallas kernels: 0 us -> 44.2 us
  between operations: 15.2 us -> 0.65 us
  matrix products: 6.15 us -> 0 us
  other arithmetic: 5.56 us -> 1.53 us
    psum x3 -> x0, waiting for transfers between devices: 165 us -> none  [the longest x1 133 us: total_terms(): return lax.psum(stacked, ('prow', 'pcol'))]
    all_gather x2 -> x0, blocking collectives: 64.4 us -> none  [the longest x1 33.2 us: on_device(): lax.all_gather(panel_parent, 'pcol', axis=1, tiled=True)]
    pallas_call x0 -> x1, Pallas kernels: none -> 44.2 us  [fused(): pl.pallas_call(functools.partial(kernel, rows, cols), out_shape=(wide,) *...]
    dot_general x8 -> x0, matrix products: 6.15 us -> none  [the longest x4 3.61 us: lead_product(): lax.dot_general(left, right, (((0,), (0,)), ((), ())), precision=highest,...]
    unnamed x21 -> x13, local copies, waits for them, and re-layouts: 1.66 us -> 4.72 us
  transfers between devices with their start and end apart: 3 -> 0, of which waited for: 2 -> 0; matrix products, arithmetic and copies ran while one was open for 2% -> 0% of each run, Pallas kernels for 0% -> 0%
where the time goes in v1:
time: 51.5 us; the launch traced here: 51.1 us
  Pallas kernels  44.2 us (86%)
  local copies, waits for them, and re-layouts  4.72 us (9%)
  other arithmetic  1.53 us (3%)
  between operations  0.65 us (1%)
    pallas_call x1, Pallas kernels, fused(): pl.pallas_call(functools.partial(kernel, rows, cols), out_shape=(wide,) *...  44.2 us
    unnamed x13, local copies, waits for them, and re-layouts  4.72 us
    another operation x1, other arithmetic, fused(): piece = jnp.stack([parent.T, child.T])  1.53 us

profile of v1, /device:TPU:0, one launch (start us, length us, event | category | flops | bytes accessed | tf_op | source)
XLA Modules:
  0.0 51.1 jit_solution(8403086072210387720)
XLA Ops:
  0.6 1.5 %pad_maximum_fusion.piece = f32[2,32,512]{2,1,0:T(8,128)} fusion(f32[1,32,512]{2,1,0:T(8,128)} %bitcast.6, f32[1,32,512]{2,1,0:T(8,128)} %bitcast.7), kind=kLoop, calls=%fused_computation | loop fusion | flops 32768 | bytes 262144 | tf_op jit(solution)/shard_map/stack | solution.py:401
  2.2 44.2 %shard_map.119 = (f32[64,256]{1,0:T(8,128)}, f32[64,256]{1,0:T(8,128)}, f32[64,256]{1,0:T(8,128)}, f32[64,256]{1,0:T(8,128)}, f32[64,256]{1,0:T(8,128)}) custom-call(s32[8]{0:T(128)} %pattern_parent.1, s32[8]{0:T(128)} %pattern_child.1, f32[2,32,512]{2,1,0:T(8,128)} %pad_maximum_fusion.piece, f32[512,256]{1,0:T(8,128)} %ainv.1, f32[256,256]{1,0:T(8,128)} %link.1, ...), custom_call_target="tpu_custom_call" | custom-call | tf_op jit(solution)/shard_map/pallas_call | solution.py:408
  46.3 0.0 copy-start.3
  46.3 1.5 %copy.18 = f32[64,256]{1,0:T(8,128)} copy(f32[64,256]{1,0:T(8,128)} %get-tuple-element.10) | data formatting | bytes 131072
  47.9 0.0 copy-done.3
  47.9 0.0 copy-start.2
  47.9 0.6 %copy.19 = f32[64,256]{1,0:T(8,128)} copy(f32[64,256]{1,0:T(8,128)S(1)} %copy-done.3) | data formatting | bytes 131072
  48.5 0.2 copy-done.2
  48.7 0.0 copy-start.1
  48.7 0.6 %copy.20 = f32[64,256]{1,0:T(8,128)} copy(f32[64,256]{1,0:T(8,128)S(1)} %copy-done.2) | data formatting | bytes 131072
  49.3 0.2 copy-done.1
  49.6 0.0 copy-start
  49.6 0.6 %copy.21 = f32[64,256]{1,0:T(8,128)} copy(f32[64,256]{1,0:T(8,128)S(1)} %copy-done.1) | data formatting | bytes 131072
  50.2 0.2 copy-done
  50.4 0.6 %copy.22 = f32[64,256]{1,0:T(8,128)} copy(f32[64,256]{1,0:T(8,128)S(1)} %copy-done) | data formatting | bytes 131072
Async XLA Ops:
  46.3 1.5 %copy-start.3 = (f32[64,256]{1,0:T(8,128)S(1)}, f32[64,256]{1,0:T(8,128)}, u32[]{:S(2)}) copy-start(f32[64,256]{1,0:T(8,128)} %get-tuple-element.11) | copy-start | bytes 196612
  47.9 0.9 %copy-start.2 = (f32[64,256]{1,0:T(8,128)S(1)}, f32[64,256]{1,0:T(8,128)}, u32[]{:S(2)}) copy-start(f32[64,256]{1,0:T(8,128)} %get-tuple-element.12) | copy-start | bytes 196612
  48.7 0.9 %copy-start.1 = (f32[64,256]{1,0:T(8,128)S(1)}, f32[64,256]{1,0:T(8,128)}, u32[]{:S(2)}) copy-start(f32[64,256]{1,0:T(8,128)} %get-tuple-element.13) | copy-start | bytes 196612
  49.6 0.9 %copy-start = (f32[64,256]{1,0:T(8,128)S(1)}, f32[64,256]{1,0:T(8,128)}, u32[]{:S(2)}) copy-start(f32[64,256]{1,0:T(8,128)} %get-tuple-element.14) | copy-start | bytes 196612

commit v2 on v1

--- a/solution.py
+++ b/solution.py
@@ -124,16 +124,17 @@
     cols,
     pattern_parent,
     pattern_child,
-    piece,
+    parent_in,
+    child_in,
+    ainv_in,
+    link_in,
+    dinv_parent_in,
+    dinv_child_in,
+    results,
     ainv,
     link,
     dinv_parent,
     dinv_child,
-    row_parent,
-    diag_parent,
-    cross_child,
-    row_child,
-    diag_child,
     panel,
     block_panel,
     ainv_high,
@@ -150,6 +151,7 @@
     side_sem,
     panel_sem,
     own_sem,
+    load_sem,
     spread_sem,
     block_sem,
     share_send,
@@ -163,7 +165,7 @@
     z, x = j // 2, j % 2
     depth = cols // 2
     width = link.shape[0]
-    piece_rows = piece.shape[1]
+    piece_rows = parent_in.shape[0]
     blocks = ainv.shape[0] // width
     share = width // rows
     own = share // cols
@@ -238,8 +240,30 @@
         pl.semaphore_signal(barrier, inc=1, device_id=(i, (j + k) % cols), device_id_type=MESH)
     for k in range(1, rows):
         pl.semaphore_signal(barrier, inc=1, device_id=((i + k) % rows, j), device_id_type=MESH)
-    keep_own = pltpu.make_async_copy(piece, piece_of(z, x), own_sem)
-    keep_own.start()
+    mine_at = pl.ds(pl.multiple_of(j * piece_rows, piece_rows), piece_rows)
+    own_loads = [
+        pltpu.make_async_copy(source, panel.at[p, mine_at, :], own_sem.at[p])
+        for p, source in enumerate((parent_in, child_in))
+    ]
+    loads = [
+        pltpu.make_async_copy(source, target, load_sem.at[n])
+        for n, (source, target) in enumerate(
+            (
+                (ainv_in, ainv),
+                (link_in, link),
+                (dinv_parent_in, dinv_parent),
+                (dinv_child_in, dinv_child),
+            )
+        )
+    ]
+    for load in own_loads + loads:
+        load.start()
+    for load in own_loads:
+        load.wait()
+    pl.semaphore_wait(barrier, cols - 1 + rows - 1)
+    relay(piece_of(z, x), z, start)
+    for load in loads:
+        load.wait()
     high, low = halves(ainv[...])
     ainv_high[...] = high
     ainv_low[...] = low
@@ -247,8 +271,6 @@
         for p, pattern in enumerate((pattern_parent, pattern_child)):
             value = pattern[i * blocks + b].astype(jnp.float32)
             masks[p, :, b * width : (b + 1) * width] = jnp.full((piece_rows, width), 1.0, jnp.float32) * value
-    pl.semaphore_wait(barrier, cols - 1 + rows - 1)
-    relay(piece, z, start)
 
     def take(level, side_index):
         slot = level * 2 + side_index
@@ -273,16 +295,15 @@
     link_halves = halves(link[...])
     link_dinv[...] = product(link_halves, halves(dinv_parent[...]), 0, 0)
 
-    keep_own.wait()
     take(z, x)
     for k in range(1, depth + 1):
         if k < depth:
             level = levels[k]
-            to(piece, level, x, own_sem, (i, z * 2 + other_x)).wait_recv()
+            to(piece_of(level, x), level, x, up_sem.at[0], (i, z * 2 + other_x)).wait_recv()
             relay(piece_of(level, x), level, start)
             take(level, x)
         level = levels[k - 1]
-        to(piece, level, other_x, own_sem, (i, z * 2 + other_x)).wait_recv()
+        to(piece_of(level, x), level, other_x, up_sem.at[0], (i, z * 2 + other_x)).wait_recv()
         take(level, other_x)
 
     def share_copy(p, k):
@@ -320,8 +341,8 @@
         sums.append(-total)
     parent_sum, child_sum = sums
     parent_sum = parent_sum * parent_here
-    row_parent[...] = parent_sum
-    row_child[...] = child_sum * child_here
+    results[0] = parent_sum
+    results[3] = child_sum * child_here
 
     parent_terms = product(halves(jnp.concatenate([parent_sum, child_sum], axis=0)), parent_block, 1, 1)
     parent_terms = parent_terms * parent_here
@@ -387,30 +408,39 @@
         term_copy(k).wait_send()
     for k in range(1, cols):
         final_copy(k, (j + cols - k) % cols).wait_recv()
-    diag_parent[...] = finals[0]
-    cross_child[...] = finals[1]
-    diag_child[...] = finals[2]
+    results[1] = finals[0]
+    results[2] = finals[1]
+    results[4] = finals[2]
     for k in range(1, cols):
         final_copy(k, j).wait_send()
+
+
+def unpack(results, *outputs):
+    for n, output in enumerate(outputs):
+        output[...] = results[n]
 
 
 def fused(rows, cols, ainv, parent, child, link, dinv_parent, dinv_child, pattern_parent, pattern_child):
     width = link.shape[0]
     share = width // rows
     own = share // cols
-    piece = jnp.stack([parent.T, child.T])
-    piece_rows, height = piece.shape[1:]
+    height, piece_rows = parent.shape
     f32 = jnp.float32
     dma = pltpu.SemaphoreType.DMA
     vmem = pl.BlockSpec(memory_space=pltpu.VMEM)
     smem = pl.BlockSpec(memory_space=pltpu.SMEM)
+    anywhere = pl.BlockSpec(memory_space=pl.ANY)
     wide = jax.ShapeDtypeStruct((share, width), f32)
-    return pl.pallas_call(
+    results = pl.pallas_call(
         functools.partial(kernel, rows, cols),
-        out_shape=(wide,) * 5,
-        in_specs=[smem, smem] + [vmem] * 5,
-        out_specs=(vmem,) * 5,
+        out_shape=jax.ShapeDtypeStruct((5, share, width), f32),
+        in_specs=[smem, smem] + [anywhere] * 6,
+        out_specs=vmem,
         scratch_shapes=[
+            pltpu.VMEM((height, width), f32),
+            pltpu.VMEM((width, width), f32),
+            pltpu.VMEM((width, width), f32),
+            pltpu.VMEM((width, width), f32),
             pltpu.VMEM((2, width, height), f32),
             pltpu.VMEM((2, width, width), f32),
             pltpu.VMEM((height, width), jnp.bfloat16),
@@ -426,7 +456,8 @@
             dma((cols // 2,)),
             dma((cols // 2,)),
             dma((cols,)),
-            dma,
+            dma((2,)),
+            dma((4,)),
             dma((cols, rows - 1)),
             dma((cols,)),
             dma((2, rows - 1)),
@@ -437,7 +468,13 @@
             dma((cols - 1,)),
         ],
         compiler_params=pltpu.CompilerParams(collective_id=0, has_side_effects=True),
-    )(pattern_parent, pattern_child, piece, ainv, link, dinv_parent, dinv_child)
+    )(pattern_parent, pattern_child, parent.T, child.T, ainv, link, dinv_parent, dinv_child)
+    return pl.pallas_call(
+        unpack,
+        out_shape=(wide,) * 5,
+        in_specs=[vmem],
+        out_specs=(vmem,) * 5,
+    )(results)
 
 
 def fits(rows, cols, width):

time: 51.5 us -> 46.1 us (0.90)
  local copies, waits for them, and re-layouts: 4.72 us -> 0 us
  other arithmetic: 1.53 us -> 0 us
  Pallas kernels: 44.2 us -> 45.2 us
    unnamed x13 -> x0, local copies, waits for them, and re-layouts: 4.72 us -> none
    another operation x1 -> x0, other arithmetic: 1.53 us -> none  [fused(): piece = jnp.stack([parent.T, child.T])]
    pallas_call x1 -> x2, Pallas kernels: 44.2 us -> 45.2 us  [the longest x1 43.6 us: fused(): pl.pallas_call(functools.partial(kernel, rows, cols), out_shape=jax.Shape...]
where the time goes in v2:
time: 46.1 us; the launch traced here: 45.9 us
  Pallas kernels  45.2 us (98%)
  between operations  0.64 us (1%)
    pallas_call x1, Pallas kernels, fused(): pl.pallas_call(functools.partial(kernel, rows, cols), out_shape=jax.Shape...  43.6 us
    pallas_call x1, Pallas kernels, fused(): pl.pallas_call(unpack, out_shape=(wide,) * 5, in_specs=[vmem], out_specs=...  1.69 us

profile of v2, /device:TPU:0, one launch (start us, length us, event | category | flops | bytes accessed | tf_op | source)
XLA Modules:
  0.0 45.9 jit_solution(17928861966145458976)
XLA Ops:
  0.6 43.6 %shard_map.119.results = f32[5,64,256]{2,1,0:T(8,128)} custom-call(s32[8]{0:T(128)} %pattern_parent.1, s32[8]{0:T(128)} %pattern_child.1, f32[32,512]{1,0:T(8,128)} %bitcast.2, f32[32,512]{1,0:T(8,128)} %bitcast.3, f32[512,256]{1,0:T(8,128)} %ainv_in.1, f32[256,256]{1,0:T(8,128)} %link_in.1, f32[256,256]{1,0:T(8,128)} %dinv_parent_in.1, f32[256,256]{1,0:T(8,128)} %dinv_child_in.1), custom_call_target="tpu_custom_call" | custom-call | tf_op jit(solution)/shard_map/pallas_call | solution.py:434
  44.2 1.7 %shard_map.120 = (f32[64,256]{1,0:T(8,128)}, f32[64,256]{1,0:T(8,128)}, f32[64,256]{1,0:T(8,128)}, f32[64,256]{1,0:T(8,128)}, f32[64,256]{1,0:T(8,128)}) custom-call(f32[5,64,256]{2,1,0:T(8,128)} %shard_map.119.results), custom_call_target="tpu_custom_call" | custom-call | tf_op jit(solution)/shard_map/pallas_call | solution.py:472

commit v3 on v2

--- a/solution.py
+++ b/solution.py
@@ -216,16 +216,28 @@
     owner = j // blocks
     half = pl.multiple_of((j % blocks) * width, width)
 
-    def spread_copy(slot, k):
+    across = (i + rows // 2) % rows
+    mate = i + 1 - 2 * (i % 2)
+    passes_on = across == owner
+
+    def spread_copy(slot, k, passing=False):
         begin = pl.multiple_of(slot * piece_rows, piece_rows)
+        landing = block_panel.at[:, pl.ds(begin, piece_rows), :]
+        source = landing if passing else panel.at[:, pl.ds(begin, piece_rows), pl.ds(half, width)]
         return pltpu.make_async_remote_copy(
-            src_ref=panel.at[:, pl.ds(begin, piece_rows), pl.ds(half, width)],
-            dst_ref=block_panel.at[:, pl.ds(begin, piece_rows), :],
+            src_ref=source,
+            dst_ref=landing,
             send_sem=spread_sem.at[slot, k],
             recv_sem=block_sem.at[slot],
-            device_id=((i + 1 + k) % rows, j),
+            device_id=((across, mate)[k], j),
             device_id_type=MESH,
         )
+
+    def pass_on(slot):
+        @pl.when(passes_on)
+        def _():
+            keep_copy(slot).wait()
+            spread_copy(slot, 1, passing=True).start()
 
     def keep_copy(slot):
         begin = pl.multiple_of(slot * piece_rows, piece_rows)
@@ -272,14 +284,20 @@
             value = pattern[i * blocks + b].astype(jnp.float32)
             masks[p, :, b * width : (b + 1) * width] = jnp.full((piece_rows, width), 1.0, jnp.float32) * value
 
+    taken = []
+
     def take(level, side_index):
         slot = level * 2 + side_index
+        taken.append(slot)
 
         @pl.when(i == owner)
         def _():
-            for k in range(rows - 1):
+            for k in range(2):
                 spread_copy(slot, k).start()
             keep_copy(slot).start()
+
+        if len(taken) > 2:
+            pass_on(taken[-3])
 
         begin = pl.multiple_of(slot * piece_rows, piece_rows)
         value = panel[:, pl.ds(begin, piece_rows), :] * masks[...]
@@ -324,73 +342,88 @@
     for k in (2, 1, 3):
         share_copy(1, k).start()
 
+    for slot in taken[-2:]:
+        pass_on(slot)
+
     parent_here = pattern_parent[j].astype(jnp.float32)
     child_here = pattern_child[j].astype(jnp.float32)
-    for slot in range(cols):
-        keep_copy(slot).wait()
+
+    @pl.when(jnp.logical_not(passes_on))
+    def _():
+        for slot in range(cols):
+            keep_copy(slot).wait()
+
     parent_block = halves(block_panel[0])
     child_block = halves(block_panel[1])
-
     mine = pl.multiple_of(i * share, share)
-    sums = []
-    for p in range(2):
+    begin = pl.multiple_of(j * own, own)
+    place = pl.multiple_of(mine + begin, own)
+    groups = ((0, 1), (1, 3))
+
+    def share_total(p):
         total = partial[p, pl.ds(mine, share), :]
         for k in range(1, rows):
             share_copy(p, k).wait_recv()
             total = total + arrived[p, k - 1]
-        sums.append(-total)
-    parent_sum, child_sum = sums
-    parent_sum = parent_sum * parent_here
-    results[0] = parent_sum
-    results[3] = child_sum * child_here
-
-    parent_terms = product(halves(jnp.concatenate([parent_sum, child_sum], axis=0)), parent_block, 1, 1)
-    parent_terms = parent_terms * parent_here
-    child_terms = product(halves(child_sum), child_block, 1, 1) * child_here
-    terms[0] = parent_terms[:share]
-    terms[1] = parent_terms[share:]
-    terms[2] = child_terms
-
-    def term_copy(k):
+        return -total
+
+    def term_copy(g, k):
+        first, last = groups[g]
         target = (j + k) % cols
-        begin = pl.multiple_of(target * own, own)
+        at = pl.multiple_of(target * own, own)
         return pltpu.make_async_remote_copy(
-            src_ref=terms.at[:, pl.ds(begin, own), :],
-            dst_ref=term_slots.at[k - 1],
-            send_sem=term_send.at[k - 1],
-            recv_sem=term_recv.at[k - 1],
+            src_ref=terms.at[first:last, pl.ds(at, own), :],
+            dst_ref=term_slots.at[k - 1, first:last],
+            send_sem=term_send.at[g, k - 1],
+            recv_sem=term_recv.at[g, k - 1],
             device_id=(i, target),
             device_id_type=MESH,
         )
 
-    for k in range(1, cols):
-        term_copy(k).start()
-    begin = pl.multiple_of(j * own, own)
-    place = pl.multiple_of(mine + begin, own)
-    total = terms[:, pl.ds(begin, own), :]
-    for k in range(1, cols):
-        term_copy(k).wait_recv()
-        total = total + term_slots[k - 1]
-    cross = -(link_dinv[pl.ds(place, own), :] + total[1])
-    finals[0, pl.ds(begin, own), :] = dinv_parent[pl.ds(place, own), :] - total[0]
-    finals[1, pl.ds(begin, own), :] = cross
-    finals[2, pl.ds(begin, own), :] = (
-        dinv_child[pl.ds(place, own), :] - product(halves(cross), link_halves, 1, 0) - total[2]
-    )
-
-    def final_copy(k, origin):
-        at = finals.at[:, pl.ds(pl.multiple_of(origin * own, own), own), :]
+    def term_total(g):
+        first, last = groups[g]
+        total = terms[first:last, pl.ds(begin, own), :]
+        for k in range(1, cols):
+            term_copy(g, k).wait_recv()
+            total = total + term_slots[k - 1, first:last]
+        return total
+
+    def final_copy(g, k, origin):
+        first, last = groups[g]
+        at = finals.at[first:last, pl.ds(pl.multiple_of(origin * own, own), own), :]
         return pltpu.make_async_remote_copy(
             src_ref=at,
             dst_ref=at,
-            send_sem=final_send.at[k - 1],
-            recv_sem=final_recv.at[k - 1],
+            send_sem=final_send.at[g, k - 1],
+            recv_sem=final_recv.at[g, k - 1],
             device_id=(i, (j + k) % cols),
             device_id_type=MESH,
         )
 
+    parent_sum = share_total(0) * parent_here
+    terms[0] = product(halves(parent_sum), parent_block, 1, 1) * parent_here
     for k in range(1, cols):
-        final_copy(k, j).start()
+        term_copy(0, k).start()
+    results[0] = parent_sum
+    child_sum = share_total(1)
+    child_halves = halves(child_sum)
+    terms[1] = product(child_halves, parent_block, 1, 1) * parent_here
+    terms[2] = product(child_halves, child_block, 1, 1) * child_here
+    for k in range(1, cols):
+        term_copy(1, k).start()
+    results[3] = child_sum * child_here
+
+    finals[0, pl.ds(begin, own), :] = dinv_parent[pl.ds(place, own), :] - term_total(0)[0]
+    for k in range(1, cols):
+        final_copy(0, k, j).start()
+    total = term_total(1)
+    cross = -(link_dinv[pl.ds(place, own), :] + total[0])
+    finals[1, pl.ds(begin, own), :] = cross
+    finals[2, pl.ds(begin, own), :] = (
+        dinv_child[pl.ds(place, own), :] - product(halves(cross), link_halves, 1, 0) - total[1]
+    )
+    for k in range(1, cols):
+        final_copy(1, k, j).start()
 
     for k in range(depth):
         relay(piece_of(levels[k], x), levels[k], lambda copy: copy.wait_send())
@@ -398,21 +431,28 @@
     @pl.when(i == owner)
     def _():
         for slot in range(cols):
-            for k in range(rows - 1):
+            for k in range(2):
                 spread_copy(slot, k).wait_send()
+
+    @pl.when(passes_on)
+    def _():
+        for slot in range(cols):
+            spread_copy(slot, 1, passing=True).wait_send()
 
     for p in range(2):
         for k in range(1, rows):
             share_copy(p, k).wait_send()
-    for k in range(1, cols):
-        term_copy(k).wait_send()
-    for k in range(1, cols):
-        final_copy(k, (j + cols - k) % cols).wait_recv()
-    results[1] = finals[0]
-    results[2] = finals[1]
-    results[4] = finals[2]
-    for k in range(1, cols):
-        final_copy(k, j).wait_send()
+    for g in range(2):
+        for k in range(1, cols):
+            term_copy(g, k).wait_send()
+    for g in range(2):
+        for k in range(1, cols):
+            final_copy(g, k, (j + cols - k) % cols).wait_recv()
+    for n, place_out in enumerate((1, 2, 4)):
+        results[place_out] = finals[n]
+    for g in range(2):
+        for k in range(1, cols):
+            final_copy(g, k, j).wait_send()
 
 
 def unpack(results, *outputs):
@@ -458,14 +498,14 @@
             dma((cols,)),
             dma((2,)),
             dma((4,)),
-            dma((cols, rows - 1)),
+            dma((cols, 2)),
             dma((cols,)),
             dma((2, rows - 1)),
             dma((2, rows - 1)),
-            dma((cols - 1,)),
-            dma((cols - 1,)),
-            dma((cols - 1,)),
-            dma((cols - 1,)),
+            dma((2, cols - 1)),
+            dma((2, cols - 1)),
+            dma((2, cols - 1)),
+            dma((2, cols - 1)),
         ],
         compiler_params=pltpu.CompilerParams(collective_id=0, has_side_effects=True),
     )(pattern_parent, pattern_child, parent.T, child.T, ainv, link, dinv_parent, dinv_child)
@@ -478,7 +518,7 @@
 
 
 def fits(rows, cols, width):
-    return cols == 8 and width % (rows * cols * 8) == 0
+    return rows == 4 and cols == 8 and width % (rows * cols * 8) == 0
 
 
 def solution(mesh):

time: 46.1 us -> 45.1 us (0.978)
  Pallas kernels: 45.2 us -> 44.2 us
    pallas_call x1, Pallas kernels: 43.6 us -> 42.5 us  [fused(): pl.pallas_call(functools.partial(kernel, rows, cols), out_shape=jax.Shape...]
where the time goes in v3:
time: 45.1 us; the launch traced here: 44.9 us
  Pallas kernels  44.2 us (98%)
  between operations  0.64 us (1%)
    pallas_call x1, Pallas kernels, fused(): pl.pallas_call(functools.partial(kernel, rows, cols), out_shape=jax.Shape...  42.5 us
    pallas_call x1, Pallas kernels, fused(): pl.pallas_call(unpack, out_shape=(wide,) * 5, in_specs=[vmem], out_specs=...  1.69 us

profile of v3, /device:TPU:0, one launch (start us, length us, event | category | flops | bytes accessed | tf_op | source)
XLA Modules:
  0.0 44.9 jit_solution(11287115048577926310)
XLA Ops:
  0.6 42.5 %shard_map.119.results = f32[5,64,256]{2,1,0:T(8,128)} custom-call(s32[8]{0:T(128)} %pattern_parent.1, s32[8]{0:T(128)} %pattern_child.1, f32[32,512]{1,0:T(8,128)} %bitcast.2, f32[32,512]{1,0:T(8,128)} %bitcast.3, f32[512,256]{1,0:T(8,128)} %ainv_in.1, f32[256,256]{1,0:T(8,128)} %link_in.1, f32[256,256]{1,0:T(8,128)} %dinv_parent_in.1, f32[256,256]{1,0:T(8,128)} %dinv_child_in.1), custom_call_target="tpu_custom_call" | custom-call | tf_op jit(solution)/shard_map/pallas_call | solution.py:474
  43.2 1.7 %shard_map.120 = (f32[64,256]{1,0:T(8,128)}, f32[64,256]{1,0:T(8,128)}, f32[64,256]{1,0:T(8,128)}, f32[64,256]{1,0:T(8,128)}, f32[64,256]{1,0:T(8,128)}) custom-call(f32[5,64,256]{2,1,0:T(8,128)} %shard_map.119.results), custom_call_target="tpu_custom_call" | custom-call | tf_op jit(solution)/shard_map/pallas_call | solution.py:512

commit v4 on v3

--- a/solution.py
+++ b/solution.py
@@ -324,24 +324,32 @@
         to(piece_of(level, x), level, other_x, up_sem.at[0], (i, z * 2 + other_x)).wait_recv()
         take(level, other_x)
 
-    def share_copy(p, k):
-        target = (i + k) % rows
-        begin = pl.multiple_of(target * share, share)
+    def rows_of(device):
+        return pl.ds(pl.multiple_of(device * share, share), share)
+
+    def share_copy(p, n):
+        source = ((mate + rows // 2) % rows, mate, across)[n]
         return pltpu.make_async_remote_copy(
-            src_ref=partial.at[p, pl.ds(begin, share), :],
-            dst_ref=arrived.at[p, k - 1],
-            send_sem=share_send.at[p, k - 1],
-            recv_sem=share_recv.at[p, k - 1],
-            device_id=(target, j),
+            src_ref=partial.at[p, rows_of(source), :],
+            dst_ref=arrived.at[p, n],
+            send_sem=share_send.at[p, n],
+            recv_sem=share_recv.at[p, n],
+            device_id=((mate, mate, across)[n], j),
             device_id_type=MESH,
         )
 
-    for k in (2, 1, 3):
-        share_copy(0, k).start()
+    def cross_over(p):
+        share_copy(p, 0).wait_recv()
+        partial[p, rows_of(across), :] = partial[p, rows_of(across), :] + arrived[p, 0]
+        share_copy(p, 2).start()
+
+    for n in range(2):
+        share_copy(0, n).start()
     partial[1] = partial[1] - product(link_halves, halves(partial[0]), 0, 0)
-    for k in (2, 1, 3):
-        share_copy(1, k).start()
-
+    for n in range(2):
+        share_copy(1, n).start()
+    for p in range(2):
+        cross_over(p)
     for slot in taken[-2:]:
         pass_on(slot)
 
@@ -362,9 +370,9 @@
 
     def share_total(p):
         total = partial[p, pl.ds(mine, share), :]
-        for k in range(1, rows):
-            share_copy(p, k).wait_recv()
-            total = total + arrived[p, k - 1]
+        for n in range(1, rows - 1):
+            share_copy(p, n).wait_recv()
+            total = total + arrived[p, n]
         return -total
 
     def term_copy(g, k):
@@ -440,8 +448,8 @@
             spread_copy(slot, 1, passing=True).wait_send()
 
     for p in range(2):
-        for k in range(1, rows):
-            share_copy(p, k).wait_send()
+        for n in range(rows - 1):
+            share_copy(p, n).wait_send()
     for g in range(2):
         for k in range(1, cols):
             term_copy(g, k).wait_send()

time: 45.1 us -> 45.8 us (1.016)
  Pallas kernels: 44.2 us -> 45 us
    pallas_call x1, Pallas kernels: 42.5 us -> 43.3 us  [fused(): pl.pallas_call(functools.partial(kernel, rows, cols), out_shape=jax.Shape...]
where the time goes in v4:
time: 45.8 us; the launch traced here: 45.6 us
  Pallas kernels  45 us (98%)
  between operations  0.64 us (1%)
    pallas_call x1, Pallas kernels, fused(): pl.pallas_call(functools.partial(kernel, rows, cols), out_shape=jax.Shape...  43.3 us
    pallas_call x1, Pallas kernels, fused(): pl.pallas_call(unpack, out_shape=(wide,) * 5, in_specs=[vmem], out_specs=...  1.69 us

profile of v4, /device:TPU:0, one launch (start us, length us, event | category | flops | bytes accessed | tf_op | source)
XLA Modules:
  0.0 45.6 jit_solution(6294188629102166940)
XLA Ops:
  0.6 43.3 %shard_map.119.results = f32[5,64,256]{2,1,0:T(8,128)} custom-call(s32[8]{0:T(128)} %pattern_parent.1, s32[8]{0:T(128)} %pattern_child.1, f32[32,512]{1,0:T(8,128)} %bitcast.2, f32[32,512]{1,0:T(8,128)} %bitcast.3, f32[512,256]{1,0:T(8,128)} %ainv_in.1, f32[256,256]{1,0:T(8,128)} %link_in.1, f32[256,256]{1,0:T(8,128)} %dinv_parent_in.1, f32[256,256]{1,0:T(8,128)} %dinv_child_in.1), custom_call_target="tpu_custom_call" | custom-call | tf_op jit(solution)/shard_map/pallas_call | solution.py:482
  43.9 1.7 %shard_map.120 = (f32[64,256]{1,0:T(8,128)}, f32[64,256]{1,0:T(8,128)}, f32[64,256]{1,0:T(8,128)}, f32[64,256]{1,0:T(8,128)}, f32[64,256]{1,0:T(8,128)}) custom-call(f32[5,64,256]{2,1,0:T(8,128)} %shard_map.119.results), custom_call_target="tpu_custom_call" | custom-call | tf_op jit(solution)/shard_map/pallas_call | solution.py:520
